TPU v7x, 32 devices: a whole 2x2x4 slice. The times are simulated.
32 devices in a mesh: blk: 16 (over z, y, x), col: 2 (over core).
Axes of the slice: x: 2, y: 2, z: 4, core: 2. Of those that a mesh axis runs over, the one named last changes fastest.
Arguments:
- queries: bfloat16 [128, 16384], P('blk', 'col'), may hold values from -6 to 6
- factor: bfloat16 [16384, 1024], P('col', 'blk'), may hold values from -0.046875 to 0.046875
- eigenvalues: float32 [1024], replicated, may hold values from 0.05 to 20
- damping: float32 [1], replicated, may hold values from 0.5 to 2
- train_rows: bfloat16 [16384, 16384], P('blk', 'col'), may hold values from -0.046875 to 0.046875
Outputs:
- scores: bfloat16 [128, 16384], P('col', 'blk')
All inputs are finite; a program needn't handle non-finite values.
Results may differ from a plain program's by a relative error of at most 0.0049.
Values may be sent and summed in bfloat16 or wider, within the bound.
A program may use at most 64 MiB of HBM per device.

v0:
```python
import jax
import jax.numpy as jnp
from jax import lax
from jax.sharding import PartitionSpec as P


def per_device(queries, factor, eigenvalues, damping, train_rows):
    damp_value = damping[0]
    weights = eigenvalues / (eigenvalues + damp_value)
    query_part = lax.all_to_all(queries, "blk", split_axis=1, concat_axis=0, tiled=True)
    factor_part = lax.all_to_all(factor, "blk", split_axis=0, concat_axis=1, tiled=True)
    partial_value = jnp.dot(query_part, factor_part, preferred_element_type=jnp.float32)
    coefficient = lax.psum(partial_value, ("blk", "col"))
    scaled = coefficient * weights[None, :]
    correction = jnp.dot(scaled, factor_part.astype(jnp.float32).T, precision=lax.Precision.HIGHEST)
    pre_part = ((query_part.astype(jnp.float32) - correction) / damp_value).astype(jnp.bfloat16)
    pre_all = lax.all_gather(pre_part, "blk", axis=1, tiled=True)
    partial_scores = jnp.einsum(
        "qk,nk->qn", pre_all, train_rows, preferred_element_type=jnp.float32
    )
    scores = lax.psum_scatter(partial_scores, "col", scatter_dimension=0, tiled=True)
    return scores.astype(jnp.bfloat16)


def solution(mesh):
    in_specs = (P("blk", "col"), P("col", "blk"), P(), P(), P("blk", "col"))
    out_specs = P("col", "blk")
    return jax.shard_map(
        per_device, mesh=mesh, in_specs=in_specs, out_specs=out_specs, check_vma=False
    )
```

profile of v0, /device:TPU:0, one launch (start us, length us, event | category | flops | bytes accessed | tf_op | source)
XLA Modules:
  0.0 269.8 jit_solution(12998497539709083565)
XLA Ops:
  6.5 8.3 %all-to-all-start = ((bf16[8,16,512]{2,0,1:T(8,128)(2,1)}), bf16[8,16,512]{2,0,1:T(8,128)(2,1)S(1)}, u32[]{:S(2)}, u32[]{:S(2)}) async-start(bf16[8,16,512]{2,0,1:T(8,128)(2,1)} %bitcast.25), calls=%async_computation | async-start | bytes 262144 | tf_op jit(solution)/shard_map/all_to_all | solution.py:10
  14.9 0.0 all-reduce.2.cloned.1.call-start
  14.9 1.3 copy.10
  16.3 6.4 %all-to-all-done = bf16[8,16,512]{2,0,1:T(8,128)(2,1)S(1)} async-done(((bf16[8,16,512]{2,0,1:T(8,128)(2,1)}), bf16[8,16,512]{2,0,1:T(8,128)(2,1)S(1)}, u32[]{:S(2)}, u32[]{:S(2)}) %all-to-all-start) | async-done | bytes 131104 | tf_op jit(solution)/shard_map/all_to_all | solution.py:10
  22.7 28.3 %all_to_all.38 = bf16[16,512,64]{1,2,0:T(8,128)(2,1)S(1)} all-to-all(bf16[16,512,64]{1,2,0:T(8,128)(2,1)S(1)} %bitcast.21), channel_id=1, replica_groups=mesh['blk'=16,'col'=2] {'blk'}, dimensions={0} | all-to-all | bytes 2097152 | tf_op jit(solution)/shard_map/all_to_all | solution.py:11
  51.0 1.3 fusion.4
  52.3 0.0 all-reduce.2.cloned.1.call-update
  52.3 0.0 all-gather.2.cloned.1.call-start
  53.0 0.7 add_divide_fusion
  53.7 126.2 %all-reduce.2.cloned.1.call-done = f32[128,1024]{1,0:T(8,128)} async-done(((f32[128,1024]{1,0:T(8,128)}), f32[128,1024]{1,0:T(8,128)}) %all-reduce.2.cloned.1.call-update) | async-done | bytes 524304 | tf_op jit(solution)/shard_map/psum | solution.py:13
  179.9 2.3 fusion.1
  182.2 0.0 all-gather.2.cloned.1.call-update
  182.2 0.0 reduce-scatter.2.cloned.1.call-start
  182.2 60.3 %all-gather.2.cloned.1.call-done = bf16[128,8192]{1,0:T(8,128)(2,1)} async-done(((bf16[128,512]{1,0:T(8,128)(2,1)}), bf16[128,8192]{1,0:T(8,128)(2,1)}) %all-gather.2.cloned.1.call-update) | async-done | bytes 2097168 | tf_op jit(solution)/shard_map/all_gather | solution.py:17
  242.5 12.9 %fusion.6 = f32[128,1024]{1,0:T(8,128)} fusion(bf16[128,8192]{1,0:T(8,128)(2,1)} %all-gather.2.cloned.1.call-done, bf16[1024,8192]{1,0:T(8,128)(2,1)} %param.9), kind=kOutput, calls=%fused_computation.9 | convolution fusion | flops 2147483648 | bytes 19398656 | tf_op jit(solution)/shard_map/qk,nk->qn/dot_general | solution.py:18
  255.4 0.0 reduce-scatter.2.cloned.1.call-update
  255.4 6.3 %reduce-scatter.2.cloned.1.call-done = f32[64,1024]{1,0:T(8,128)} async-done(((f32[128,1024]{1,0:T(8,128)}), f32[64,1024]{1,0:T(8,128)}) %reduce-scatter.2.cloned.1.call-update) | async-done | bytes 262160 | tf_op jit(solution)/shard_map/reduce_scatter | solution.py:21
  261.7 1.6 convert_element_type.12
Async XLA Ops:
  6.5 16.1 %all-to-all-start = ((bf16[8,16,512]{2,0,1:T(8,128)(2,1)}), bf16[8,16,512]{2,0,1:T(8,128)(2,1)S(1)}, u32[]{:S(2)}, u32[]{:S(2)}) async-start(bf16[8,16,512]{2,0,1:T(8,128)(2,1)} %bitcast.25), calls=%async_computation | async-start | bytes 262144 | tf_op jit(solution)/shard_map/all_to_all | solution.py:10
  14.9 165.0 %all-reduce.2.cloned.1.call-start = ((), (), s32[]{:S(2)}) async-start(), calls=%async_computation.3 | async-start | bytes 1048576 | tf_op jit(solution)/shard_map/psum | solution.py:13
  52.3 190.2 %all-gather.2.cloned.1.call-start = ((), (), s32[]{:S(2)}) async-start(), calls=%async_computation.4 | async-start | bytes 2228224 | tf_op jit(solution)/shard_map/all_gather | solution.py:17
  182.2 79.5 %reduce-scatter.2.cloned.1.call-start = ((), (), s32[]{:S(2)}) async-start(), calls=%async_computation.5 | async-start | bytes 786432 | tf_op jit(solution)/shard_map/reduce_scatter | solution.py:21
Sparse Core Ops, SparseCore 0:
  52.4 127.3 all-reduce.1
  182.6 59.8 all-gather.1
  255.6 6.0 reduce-scatter.1
where the time goes:
time: 270 us
  waiting for transfers between devices  199 us (74%)
  blocking collectives  28.3 us (10%)
  matrix products  16.4 us (6%)
  between operations  13.8 us (5%)
  starting transfers between devices  8.47 us (3%)
    psum x1, waiting for transfers between devices, per_device(): coefficient = lax.psum(partial_value, ('blk', 'col'))  126 us
    all_gather x1, waiting for transfers between devices, per_device(): pre_all = lax.all_gather(pre_part, 'blk', axis=1, tiled=True)  60.3 us
    all_to_all x1, blocking collectives, per_device(): lax.all_to_all(factor, 'blk', split_axis=0, concat_axis=1, tiled=True)  28.3 us
    dot_general x1, matrix products, per_device(): jnp.einsum('qk,nk->qn', pre_all, train_rows, preferred_element_type=jnp.f...  12.9 us
    all_to_all x1, starting transfers between devices, per_device(): lax.all_to_all(queries, 'blk', split_axis=1, concat_axis=0, tiled=True)  8.34 us
    all_to_all x1, waiting for transfers between devices, per_device(): lax.all_to_all(queries, 'blk', split_axis=1, concat_axis=0, tiled=True)  6.41 us
    reduce_scatter x1, waiting for transfers between devices, per_device(): lax.psum_scatter(partial_scores, 'col', scatter_dimension=0, tiled=True)  6.26 us
  transfers between devices with their start and end apart: 4, of which 4 were waited for; matrix products, arithmetic and copies ran while one was open for 1% of the time, Pallas kernels for 0%

commit v1 on v0

--- a/solution.py
+++ b/solution.py
@@ -14,10 +14,28 @@
     scaled = coefficient * weights[None, :]
     correction = jnp.dot(scaled, factor_part.astype(jnp.float32).T, precision=lax.Precision.HIGHEST)
     pre_part = ((query_part.astype(jnp.float32) - correction) / damp_value).astype(jnp.bfloat16)
-    pre_all = lax.all_gather(pre_part, "blk", axis=1, tiled=True)
+    field_out, t_next = (lax.axis_size("blk"), lax.axis_index("blk"))
+    made = []
+    for k0 in range(field_out):
+        made.append((k0, (k0 - 1) % field_out))
+    current_value = pre_part.shape[1]
+    before = pre_part
     partial_scores = jnp.einsum(
-        "qk,nk->qn", pre_all, train_rows, preferred_element_type=jnp.float32
+        "qk,nk->qn",
+        before,
+        lax.dynamic_slice_in_dim(train_rows, t_next * current_value, before.shape[1], axis=1),
+        preferred_element_type=jnp.float32,
     )
+    for t in range(1, field_out):
+        before = lax.ppermute(before, "blk", made)
+        partial_scores = partial_scores + jnp.einsum(
+            "qk,nk->qn",
+            before,
+            lax.dynamic_slice_in_dim(
+                train_rows, (t_next + t) % field_out * current_value, before.shape[1], axis=1
+            ),
+            preferred_element_type=jnp.float32,
+        )
     scores = lax.psum_scatter(partial_scores, "col", scatter_dimension=0, tiled=True)
     return scores.astype(jnp.bfloat16)
 

time: 270 us -> 331 us (1.23)
  starting transfers between devices: 8.47 us -> 96.5 us
  waiting for transfers between devices: 199 us -> 168 us
  matrix products: 16.4 us -> 20.1 us
    ppermute x0 -> x15, starting transfers between devices: none -> 88 us  [per_device(): before = lax.ppermute(before, 'blk', made)]
    all_gather x1 -> x0, waiting for transfers between devices: 60.3 us -> none  [per_device(): pre_all = lax.all_gather(pre_part, 'blk', axis=1, tiled=True)]
    ppermute x0 -> x15, waiting for transfers between devices: none -> 25.4 us  [per_device(): before = lax.ppermute(before, 'blk', made)]
    dot_general x1 -> x16, matrix products: 12.9 us -> 17 us  [the longest x15 15.3 us: per_device(): jnp.einsum('qk,nk->qn', before, lax.dynamic_slice_in_dim(train_rows, (t_n...]
    reduce_scatter x1, waiting for transfers between devices: 6.26 us -> 9.9 us  [per_device(): lax.psum_scatter(partial_scores, 'col', scatter_dimension=0, tiled=True)]
  transfers between devices with their start and end apart: 4 -> 18, of which waited for: 4 -> 18; matrix products, arithmetic and copies ran while one was open for 1% -> 5% of each run, Pallas kernels for 0% -> 0%
where the time goes in v1:
time: 331 us
  waiting for transfers between devices  168 us (51%)
  starting transfers between devices  96.5 us (29%)
  blocking collectives  28.3 us (9%)
  matrix products  20.1 us (6%)
  between operations  14.4 us (4%)
    psum x1, waiting for transfers between devices, per_device(): coefficient = lax.psum(partial_value, ('blk', 'col'))  126 us
    ppermute x15, starting transfers between devices, per_device(): before = lax.ppermute(before, 'blk', made)  88 us
    all_to_all x1, blocking collectives, per_device(): lax.all_to_all(factor, 'blk', split_axis=0, concat_axis=1, tiled=True)  28.3 us
    ppermute x15, waiting for transfers between devices, per_device(): before = lax.ppermute(before, 'blk', made)  25.4 us
    dot_general x15, matrix products, per_device(): jnp.einsum('qk,nk->qn', before, lax.dynamic_slice_in_dim(train_rows, (t_n...  15.3 us
    reduce_scatter x1, waiting for transfers between devices, per_device(): lax.psum_scatter(partial_scores, 'col', scatter_dimension=0, tiled=True)  9.9 us
    all_to_all x1, starting transfers between devices, per_device(): lax.all_to_all(queries, 'blk', split_axis=1, concat_axis=0, tiled=True)  8.34 us
  transfers between devices with their start and end apart: 18, of which 18 were waited for; matrix products, arithmetic and copies ran while one was open for 5% of the time, Pallas kernels for 0%

profile of v1, /device:TPU:0, one launch (start us, length us, event | category | flops | bytes accessed | tf_op | source)
XLA Modules:
  0.0 330.7 jit_solution(13616123613609775824)
XLA Ops:
  6.5 8.3 %all-to-all-start = ((bf16[8,16,512]{2,0,1:T(8,128)(2,1)}), bf16[8,16,512]{2,0,1:T(8,128)(2,1)S(1)}, u32[]{:S(2)}, u32[]{:S(2)}) async-start(bf16[8,16,512]{2,0,1:T(8,128)(2,1)} %bitcast.39), calls=%async_computation | async-start | bytes 262144 | tf_op jit(solution)/shard_map/all_to_all | solution.py:10
  16.3 6.4 %all-to-all-done = bf16[8,16,512]{2,0,1:T(8,128)(2,1)S(1)} async-done(((bf16[8,16,512]{2,0,1:T(8,128)(2,1)}), bf16[8,16,512]{2,0,1:T(8,128)(2,1)S(1)}, u32[]{:S(2)}, u32[]{:S(2)}) %all-to-all-start) | async-done | bytes 131104 | tf_op jit(solution)/shard_map/all_to_all | solution.py:10
  22.7 28.3 %all_to_all.38 = bf16[16,512,64]{1,2,0:T(8,128)(2,1)S(1)} all-to-all(bf16[16,512,64]{1,2,0:T(8,128)(2,1)S(1)} %bitcast.35), channel_id=1, replica_groups=mesh['blk'=16,'col'=2] {'blk'}, dimensions={0} | all-to-all | bytes 2097152 | tf_op jit(solution)/shard_map/all_to_all | solution.py:11
  53.9 126.0 %all-reduce.2.cloned.1.call-done = f32[128,1024]{1,0:T(8,128)} async-done(((f32[128,1024]{1,0:T(8,128)}), f32[128,1024]{1,0:T(8,128)}) %all-reduce.2.cloned.1.call-update) | async-done | bytes 524304 | tf_op jit(solution)/shard_map/psum | solution.py:13
  181.7 3.3 collective-permute-start
  187.5 6.0 %collective-permute-start.1 = (bf16[128,512]{1,0:T(8,128)(2,1)S(1)}, bf16[128,512]{1,0:T(8,128)(2,1)S(1)}, u32[]{:S(2)}, u32[]{:S(2)}) collective-permute-start(bf16[128,512]{1,0:T(8,128)(2,1)S(1)} %collective-permute-done), channel_id=1, source_target_pairs={{0,30},{2,0},{4,2},{6,4},{8,6},{10,8},{12,10},{14,12},{16,14},{18,... | collective-permute-start | bytes 393224 | tf_op jit(solution)/shard_map/ppermute | solution.py:30
  196.1 6.0 %collective-permute-start.2 = (bf16[128,512]{1,0:T(8,128)(2,1)S(1)}, bf16[128,512]{1,0:T(8,128)(2,1)S(1)}, u32[]{:S(2)}, u32[]{:S(2)}) collective-permute-start(bf16[128,512]{1,0:T(8,128)(2,1)S(1)} %collective-permute-done.1), channel_id=1, source_target_pairs={{0,30},{2,0},{4,2},{6,4},{8,6},{10,8},{12,10},{14,12},{16,14},{18,... | collective-permute-start | bytes 393224 | tf_op jit(solution)/shard_map/ppermute | solution.py:30
  204.6 6.0 %collective-permute-start.3 = (bf16[128,512]{1,0:T(8,128)(2,1)S(1)}, bf16[128,512]{1,0:T(8,128)(2,1)S(1)}, u32[]{:S(2)}, u32[]{:S(2)}) collective-permute-start(bf16[128,512]{1,0:T(8,128)(2,1)S(1)} %collective-permute-done.2), channel_id=1, source_target_pairs={{0,30},{2,0},{4,2},{6,4},{8,6},{10,8},{12,10},{14,12},{16,14},{18,... | collective-permute-start | bytes 393224 | tf_op jit(solution)/shard_map/ppermute | solution.py:30
  213.2 6.0 %collective-permute-start.4 = (bf16[128,512]{1,0:T(8,128)(2,1)S(1)}, bf16[128,512]{1,0:T(8,128)(2,1)S(1)}, u32[]{:S(2)}, u32[]{:S(2)}) collective-permute-start(bf16[128,512]{1,0:T(8,128)(2,1)S(1)} %collective-permute-done.3), channel_id=1, source_target_pairs={{0,30},{2,0},{4,2},{6,4},{8,6},{10,8},{12,10},{14,12},{16,14},{18,... | collective-permute-start | bytes 393224 | tf_op jit(solution)/shard_map/ppermute | solution.py:30
  222.2 6.1 %collective-permute-start.5 = (bf16[128,512]{1,0:T(8,128)(2,1)S(1)}, bf16[128,512]{1,0:T(8,128)(2,1)S(1)}, u32[]{:S(2)}, u32[]{:S(2)}) collective-permute-start(bf16[128,512]{1,0:T(8,128)(2,1)S(1)} %collective-permute-done.4), channel_id=1, source_target_pairs={{0,30},{2,0},{4,2},{6,4},{8,6},{10,8},{12,10},{14,12},{16,14},{18,... | collective-permute-start | bytes 393224 | tf_op jit(solution)/shard_map/ppermute | solution.py:30
  231.9 6.1 %collective-permute-start.6 = (bf16[128,512]{1,0:T(8,128)(2,1)S(1)}, bf16[128,512]{1,0:T(8,128)(2,1)S(1)}, u32[]{:S(2)}, u32[]{:S(2)}) collective-permute-start(bf16[128,512]{1,0:T(8,128)(2,1)S(1)} %collective-permute-done.5), channel_id=1, source_target_pairs={{0,30},{2,0},{4,2},{6,4},{8,6},{10,8},{12,10},{14,12},{16,14},{18,... | collective-permute-start | bytes 393224 | tf_op jit(solution)/shard_map/ppermute | solution.py:30
  240.8 6.1 %collective-permute-start.7 = (bf16[128,512]{1,0:T(8,128)(2,1)S(1)}, bf16[128,512]{1,0:T(8,128)(2,1)S(1)}, u32[]{:S(2)}, u32[]{:S(2)}) collective-permute-start(bf16[128,512]{1,0:T(8,128)(2,1)S(1)} %collective-permute-done.6), channel_id=1, source_target_pairs={{0,30},{2,0},{4,2},{6,4},{8,6},{10,8},{12,10},{14,12},{16,14},{18,... | collective-permute-start | bytes 393224 | tf_op jit(solution)/shard_map/ppermute | solution.py:30
  249.4 6.0 %collective-permute-start.8 = (bf16[128,512]{1,0:T(8,128)(2,1)S(1)}, bf16[128,512]{1,0:T(8,128)(2,1)S(1)}, u32[]{:S(2)}, u32[]{:S(2)}) collective-permute-start(bf16[128,512]{1,0:T(8,128)(2,1)S(1)} %collective-permute-done.7), channel_id=1, source_target_pairs={{0,30},{2,0},{4,2},{6,4},{8,6},{10,8},{12,10},{14,12},{16,14},{18,... | collective-permute-start | bytes 393224 | tf_op jit(solution)/shard_map/ppermute | solution.py:30
  255.9 2.0 collective-permute-done.8
  257.9 6.0 %collective-permute-start.9 = (bf16[128,512]{1,0:T(8,128)(2,1)S(1)}, bf16[128,512]{1,0:T(8,128)(2,1)S(1)}, u32[]{:S(2)}, u32[]{:S(2)}) collective-permute-start(bf16[128,512]{1,0:T(8,128)(2,1)S(1)} %collective-permute-done.8), channel_id=1, source_target_pairs={{0,30},{2,0},{4,2},{6,4},{8,6},{10,8},{12,10},{14,12},{16,14},{18,... | collective-permute-start | bytes 393224 | tf_op jit(solution)/shard_map/ppermute | solution.py:30
  266.5 6.0 %collective-permute-start.10 = (bf16[128,512]{1,0:T(8,128)(2,1)S(1)}, bf16[128,512]{1,0:T(8,128)(2,1)S(1)}, u32[]{:S(2)}, u32[]{:S(2)}) collective-permute-start(bf16[128,512]{1,0:T(8,128)(2,1)S(1)} %collective-permute-done.9), channel_id=1, source_target_pairs={{0,30},{2,0},{4,2},{6,4},{8,6},{10,8},{12,10},{14,12},{16,14},{18,... | collective-permute-start | bytes 393224 | tf_op jit(solution)/shard_map/ppermute | solution.py:30
  273.0 2.0 collective-permute-done.10
  275.1 6.0 %collective-permute-start.11 = (bf16[128,512]{1,0:T(8,128)(2,1)S(1)}, bf16[128,512]{1,0:T(8,128)(2,1)S(1)}, u32[]{:S(2)}, u32[]{:S(2)}) collective-permute-start(bf16[128,512]{1,0:T(8,128)(2,1)S(1)} %collective-permute-done.10), channel_id=1, source_target_pairs={{0,30},{2,0},{4,2},{6,4},{8,6},{10,8},{12,10},{14,12},{16,14},{18,... | collective-permute-start | bytes 393224 | tf_op jit(solution)/shard_map/ppermute | solution.py:30
  281.6 2.6 collective-permute-done.11
  284.2 6.1 %collective-permute-start.12 = (bf16[128,512]{1,0:T(8,128)(2,1)S(1)}, bf16[128,512]{1,0:T(8,128)(2,1)S(1)}, u32[]{:S(2)}, u32[]{:S(2)}) collective-permute-start(bf16[128,512]{1,0:T(8,128)(2,1)S(1)} %collective-permute-done.11), channel_id=1, source_target_pairs={{0,30},{2,0},{4,2},{6,4},{8,6},{10,8},{12,10},{14,12},{16,14},{18,... | collective-permute-start | bytes 393224 | tf_op jit(solution)/shard_map/ppermute | solution.py:30
  290.7 3.1 collective-permute-done.12
  293.8 6.1 %collective-permute-start.13 = (bf16[128,512]{1,0:T(8,128)(2,1)S(1)}, bf16[128,512]{1,0:T(8,128)(2,1)S(1)}, u32[]{:S(2)}, u32[]{:S(2)}) collective-permute-start(bf16[128,512]{1,0:T(8,128)(2,1)S(1)} %collective-permute-done.12), channel_id=1, source_target_pairs={{0,30},{2,0},{4,2},{6,4},{8,6},{10,8},{12,10},{14,12},{16,14},{18,... | collective-permute-start | bytes 393224 | tf_op jit(solution)/shard_map/ppermute | solution.py:30
  302.4 6.0 %collective-permute-start.14 = (bf16[128,512]{1,0:T(8,128)(2,1)S(1)}, bf16[128,512]{1,0:T(8,128)(2,1)S(1)}, u32[]{:S(2)}, u32[]{:S(2)}) collective-permute-start(bf16[128,512]{1,0:T(8,128)(2,1)S(1)} %collective-permute-done.13), channel_id=1, source_target_pairs={{0,30},{2,0},{4,2},{6,4},{8,6},{10,8},{12,10},{14,12},{16,14},{18,... | collective-permute-start | bytes 393224 | tf_op jit(solution)/shard_map/ppermute | solution.py:30
  312.3 9.9 %reduce-scatter.2.cloned.1.call-done = f32[64,1024]{1,0:T(8,128)} async-done(((f32[128,1024]{1,0:T(8,128)}), f32[64,1024]{1,0:T(8,128)}) %reduce-scatter.2.cloned.1.call-update) | async-done | bytes 262160 | tf_op jit(solution)/shard_map/reduce_scatter | solution.py:39
  (38 shorter events, 39.5 us)
Async XLA Ops:
  6.5 16.1 %all-to-all-start = ((bf16[8,16,512]{2,0,1:T(8,128)(2,1)}), bf16[8,16,512]{2,0,1:T(8,128)(2,1)S(1)}, u32[]{:S(2)}, u32[]{:S(2)}) async-start(bf16[8,16,512]{2,0,1:T(8,128)(2,1)} %bitcast.39), calls=%async_computation | async-start | bytes 262144 | tf_op jit(solution)/shard_map/all_to_all | solution.py:10
  14.9 165.0 %all-reduce.2.cloned.1.call-start = ((), (), s32[]{:S(2)}) async-start(), calls=%async_computation.3 | async-start | bytes 1048576 | tf_op jit(solution)/shard_map/psum | solution.py:13
  52.3 269.9 %reduce-scatter.2.cloned.1.call-start = ((), (), s32[]{:S(2)}) async-start(), calls=%async_computation.4 | async-start | bytes 786432 | tf_op jit(solution)/shard_map/reduce_scatter | solution.py:39
  179.9 67.0 %copy-start = (bf16[1024,8192]{1,0:T(8,128)(2,1)S(1)}, bf16[1024,8192]{1,0:T(8,128)(2,1)}, u32[]{:S(2)}) copy-start(bf16[1024,8192]{1,0:T(8,128)(2,1)} %param.9) | copy-start | bytes 50331652
  181.7 5.8 %collective-permute-start = (bf16[128,512]{1,0:T(8,128)(2,1)S(1)}, bf16[128,512]{1,0:T(8,128)(2,1)S(1)}, u32[]{:S(2)}, u32[]{:S(2)}) collective-permute-start(bf16[128,512]{1,0:T(8,128)(2,1)S(1)} %fusion.1), channel_id=1, source_target_pairs={{0,30},{2,0},{4,2},{6,4},{8,6},{10,8},{12,10},{14,12},{16,14},{18,... | collective-permute-start | bytes 393224 | tf_op jit(solution)/shard_map/ppermute | solution.py:30
  187.5 8.6 %collective-permute-start.1 = (bf16[128,512]{1,0:T(8,128)(2,1)S(1)}, bf16[128,512]{1,0:T(8,128)(2,1)S(1)}, u32[]{:S(2)}, u32[]{:S(2)}) collective-permute-start(bf16[128,512]{1,0:T(8,128)(2,1)S(1)} %collective-permute-done), channel_id=1, source_target_pairs={{0,30},{2,0},{4,2},{6,4},{8,6},{10,8},{12,10},{14,12},{16,14},{18,... | collective-permute-start | bytes 393224 | tf_op jit(solution)/shard_map/ppermute | solution.py:30
  196.1 8.6 %collective-permute-start.2 = (bf16[128,512]{1,0:T(8,128)(2,1)S(1)}, bf16[128,512]{1,0:T(8,128)(2,1)S(1)}, u32[]{:S(2)}, u32[]{:S(2)}) collective-permute-start(bf16[128,512]{1,0:T(8,128)(2,1)S(1)} %collective-permute-done.1), channel_id=1, source_target_pairs={{0,30},{2,0},{4,2},{6,4},{8,6},{10,8},{12,10},{14,12},{16,14},{18,... | collective-permute-start | bytes 393224 | tf_op jit(solution)/shard_map/ppermute | solution.py:30
  204.6 8.6 %collective-permute-start.3 = (bf16[128,512]{1,0:T(8,128)(2,1)S(1)}, bf16[128,512]{1,0:T(8,128)(2,1)S(1)}, u32[]{:S(2)}, u32[]{:S(2)}) collective-permute-start(bf16[128,512]{1,0:T(8,128)(2,1)S(1)} %collective-permute-done.2), channel_id=1, source_target_pairs={{0,30},{2,0},{4,2},{6,4},{8,6},{10,8},{12,10},{14,12},{16,14},{18,... | collective-permute-start | bytes 393224 | tf_op jit(solution)/shard_map/ppermute | solution.py:30
  213.2 9.0 %collective-permute-start.4 = (bf16[128,512]{1,0:T(8,128)(2,1)S(1)}, bf16[128,512]{1,0:T(8,128)(2,1)S(1)}, u32[]{:S(2)}, u32[]{:S(2)}) collective-permute-start(bf16[128,512]{1,0:T(8,128)(2,1)S(1)} %collective-permute-done.3), channel_id=1, source_target_pairs={{0,30},{2,0},{4,2},{6,4},{8,6},{10,8},{12,10},{14,12},{16,14},{18,... | collective-permute-start | bytes 393224 | tf_op jit(solution)/shard_map/ppermute | solution.py:30
  222.2 9.7 %collective-permute-start.5 = (bf16[128,512]{1,0:T(8,128)(2,1)S(1)}, bf16[128,512]{1,0:T(8,128)(2,1)S(1)}, u32[]{:S(2)}, u32[]{:S(2)}) collective-permute-start(bf16[128,512]{1,0:T(8,128)(2,1)S(1)} %collective-permute-done.4), channel_id=1, source_target_pairs={{0,30},{2,0},{4,2},{6,4},{8,6},{10,8},{12,10},{14,12},{16,14},{18,... | collective-permute-start | bytes 393224 | tf_op jit(solution)/shard_map/ppermute | solution.py:30
  231.9 8.8 %collective-permute-start.6 = (bf16[128,512]{1,0:T(8,128)(2,1)S(1)}, bf16[128,512]{1,0:T(8,128)(2,1)S(1)}, u32[]{:S(2)}, u32[]{:S(2)}) collective-permute-start(bf16[128,512]{1,0:T(8,128)(2,1)S(1)} %collective-permute-done.5), channel_id=1, source_target_pairs={{0,30},{2,0},{4,2},{6,4},{8,6},{10,8},{12,10},{14,12},{16,14},{18,... | collective-permute-start | bytes 393224 | tf_op jit(solution)/shard_map/ppermute | solution.py:30
  240.8 8.6 %collective-permute-start.7 = (bf16[128,512]{1,0:T(8,128)(2,1)S(1)}, bf16[128,512]{1,0:T(8,128)(2,1)S(1)}, u32[]{:S(2)}, u32[]{:S(2)}) collective-permute-start(bf16[128,512]{1,0:T(8,128)(2,1)S(1)} %collective-permute-done.6), channel_id=1, source_target_pairs={{0,30},{2,0},{4,2},{6,4},{8,6},{10,8},{12,10},{14,12},{16,14},{18,... | collective-permute-start | bytes 393224 | tf_op jit(solution)/shard_map/ppermute | solution.py:30
  249.4 8.6 %collective-permute-start.8 = (bf16[128,512]{1,0:T(8,128)(2,1)S(1)}, bf16[128,512]{1,0:T(8,128)(2,1)S(1)}, u32[]{:S(2)}, u32[]{:S(2)}) collective-permute-start(bf16[128,512]{1,0:T(8,128)(2,1)S(1)} %collective-permute-done.7), channel_id=1, source_target_pairs={{0,30},{2,0},{4,2},{6,4},{8,6},{10,8},{12,10},{14,12},{16,14},{18,... | collective-permute-start | bytes 393224 | tf_op jit(solution)/shard_map/ppermute | solution.py:30
  257.9 8.6 %collective-permute-start.9 = (bf16[128,512]{1,0:T(8,128)(2,1)S(1)}, bf16[128,512]{1,0:T(8,128)(2,1)S(1)}, u32[]{:S(2)}, u32[]{:S(2)}) collective-permute-start(bf16[128,512]{1,0:T(8,128)(2,1)S(1)} %collective-permute-done.8), channel_id=1, source_target_pairs={{0,30},{2,0},{4,2},{6,4},{8,6},{10,8},{12,10},{14,12},{16,14},{18,... | collective-permute-start | bytes 393224 | tf_op jit(solution)/shard_map/ppermute | solution.py:30
  266.5 8.6 %collective-permute-start.10 = (bf16[128,512]{1,0:T(8,128)(2,1)S(1)}, bf16[128,512]{1,0:T(8,128)(2,1)S(1)}, u32[]{:S(2)}, u32[]{:S(2)}) collective-permute-start(bf16[128,512]{1,0:T(8,128)(2,1)S(1)} %collective-permute-done.9), channel_id=1, source_target_pairs={{0,30},{2,0},{4,2},{6,4},{8,6},{10,8},{12,10},{14,12},{16,14},{18,... | collective-permute-start | bytes 393224 | tf_op jit(solution)/shard_map/ppermute | solution.py:30
  275.1 9.1 %collective-permute-start.11 = (bf16[128,512]{1,0:T(8,128)(2,1)S(1)}, bf16[128,512]{1,0:T(8,128)(2,1)S(1)}, u32[]{:S(2)}, u32[]{:S(2)}) collective-permute-start(bf16[128,512]{1,0:T(8,128)(2,1)S(1)} %collective-permute-done.10), channel_id=1, source_target_pairs={{0,30},{2,0},{4,2},{6,4},{8,6},{10,8},{12,10},{14,12},{16,14},{18,... | collective-permute-start | bytes 393224 | tf_op jit(solution)/shard_map/ppermute | solution.py:30
  284.2 9.7 %collective-permute-start.12 = (bf16[128,512]{1,0:T(8,128)(2,1)S(1)}, bf16[128,512]{1,0:T(8,128)(2,1)S(1)}, u32[]{:S(2)}, u32[]{:S(2)}) collective-permute-start(bf16[128,512]{1,0:T(8,128)(2,1)S(1)} %collective-permute-done.11), channel_id=1, source_target_pairs={{0,30},{2,0},{4,2},{6,4},{8,6},{10,8},{12,10},{14,12},{16,14},{18,... | collective-permute-start | bytes 393224 | tf_op jit(solution)/shard_map/ppermute | solution.py:30
  293.8 8.6 %collective-permute-start.13 = (bf16[128,512]{1,0:T(8,128)(2,1)S(1)}, bf16[128,512]{1,0:T(8,128)(2,1)S(1)}, u32[]{:S(2)}, u32[]{:S(2)}) collective-permute-start(bf16[128,512]{1,0:T(8,128)(2,1)S(1)} %collective-permute-done.12), channel_id=1, source_target_pairs={{0,30},{2,0},{4,2},{6,4},{8,6},{10,8},{12,10},{14,12},{16,14},{18,... | collective-permute-start | bytes 393224 | tf_op jit(solution)/shard_map/ppermute | solution.py:30
  302.4 8.6 %collective-permute-start.14 = (bf16[128,512]{1,0:T(8,128)(2,1)S(1)}, bf16[128,512]{1,0:T(8,128)(2,1)S(1)}, u32[]{:S(2)}, u32[]{:S(2)}) collective-permute-start(bf16[128,512]{1,0:T(8,128)(2,1)S(1)} %collective-permute-done.13), channel_id=1, source_target_pairs={{0,30},{2,0},{4,2},{6,4},{8,6},{10,8},{12,10},{14,12},{16,14},{18,... | collective-permute-start | bytes 393224 | tf_op jit(solution)/shard_map/ppermute | solution.py:30
Sparse Core Ops, SparseCore 0:
  52.4 127.3 all-reduce.1
  312.4 9.7 reduce-scatter.1
